TPU v7x, 32 devices: a whole 2x2x4 slice. The times are simulated.
32 devices in a mesh: rows: 16 (over z, y, x), cols: 2 (over core).
Axes of the slice: x: 2, y: 2, z: 4, core: 2. Of those that a mesh axis runs over, the one named last changes fastest.
Arguments:
- pair_map: bfloat16 [32, 128, 2048], P(None, 'cols', 'rows'), may hold values from -44 to 44
- conv_in: bfloat16 [32, 288], replicated, may hold values from -0.375 to 0.375
- embed_weight: bfloat16 [2048, 256], replicated, may hold values from -0.125 to 0.125
- qkv_weight: bfloat16 [256, 768], replicated, may hold values from -0.5 to 0.5
- key_bias: bfloat16 [256, 16, 8], P('rows', 'cols'), may hold values from -4 to 260
- out_weight: bfloat16 [256, 256], replicated, may hold values from -0.375 to 0.375
- unpatch: bfloat16 [256, 2048], replicated, may hold values from -0.375 to 0.375
- conv_out: bfloat16 [32, 288], replicated, may hold values from -0.375 to 0.375
Outputs:
- trunk_out: bfloat16 [32, 128, 2048], P(None, 'cols', 'rows')
All inputs are finite; a program needn't handle non-finite values.
Results may differ from a plain program's by a relative error of at most 0.014.
Values may be sent and summed in bfloat16 or wider, within the bound.
A program may use at most 128 MiB of HBM per device.

v0:
```python
import jax
import jax.numpy as jnp
from jax import lax
from jax.sharding import PartitionSpec as P

C = 32
PATCH = 8
D = 256
HEADS = 8
HEAD_DIM = 32


epsilon = 1e-05


def padded_2(block, sides, width):
    for axis, dim in sides:
        count = lax.axis_size(axis)
        forward = [(i, i + 1) for i in range(count - 1)]
        backward = [(target, source) for source, target in forward]
        low = lax.ppermute(
            lax.slice_in_dim(block, block.shape[dim] - width, None, axis=dim), axis, forward
        )
        high = lax.ppermute(lax.slice_in_dim(block, 0, width, axis=dim), axis, backward)
        block = jnp.concatenate([low, block, high], axis=dim)
    return block


def conv_valid(padded, weight):
    channels = padded.shape[0]
    extent_one = padded.shape[1] - 2
    extent_two = padded.shape[2] - 2
    stacked = jnp.concatenate(
        [
            padded[:, shift_col : shift_col + extent_one, shift_row : shift_row + extent_two]
            for shift_col in range(3)
            for shift_row in range(3)
        ],
        axis=0,
    )
    product = jnp.dot(
        weight,
        stacked.reshape(9 * channels, extent_one * extent_two),
        preferred_element_type=jnp.float32,
    )
    return product.reshape(weight.shape[0], extent_one, extent_two)


def convolve(local_map, weight, fetch_rim):
    return conv_valid(fetch_rim(local_map), weight)


def fetch_input(local_map):
    return padded_2(local_map, (("rows", 2), ("cols", 1)), 1)


def fetch_output(local_map):
    return padded_2(local_map, (("rows", 2), ("cols", 1)), 1)


def layer_norm(tokens):
    values = tokens.astype(jnp.float32)
    row_mean = jnp.mean(values, axis=1, keepdims=True)
    centered = values - row_mean
    row_var = jnp.mean(centered * centered, axis=1, keepdims=True)
    return (centered * lax.rsqrt(row_var + epsilon)).astype(jnp.bfloat16)


def attend(qkv_rows, bias_row):
    seq_length = qkv_rows.shape[0]
    block_rows = min(512, seq_length)
    queries = qkv_rows[:, :HEAD_DIM]
    key_rows = qkv_rows[:, HEAD_DIM : 2 * HEAD_DIM]
    value_rows = qkv_rows[:, 2 * HEAD_DIM :]
    key_shift = bias_row.astype(jnp.float32)[None, :]
    score_scale = HEAD_DIM ** (-0.5)

    def one_block(query_block):
        scores = (
            jnp.dot(query_block, key_rows.T, preferred_element_type=jnp.float32) * score_scale
            + key_shift
        )
        row_peak = jnp.max(scores, axis=1, keepdims=True)
        weights = jnp.exp(scores - row_peak)
        soft_weights = (weights / jnp.sum(weights, axis=1, keepdims=True)).astype(jnp.bfloat16)
        return jnp.dot(soft_weights, value_rows, preferred_element_type=jnp.float32).astype(
            jnp.bfloat16
        )

    result = lax.map(one_block, queries.reshape(seq_length // block_rows, block_rows, HEAD_DIM))
    return result.reshape(seq_length, HEAD_DIM)


def attend_many(qkv_items, bias_items):

    def attend_pair(pair_item):
        return attend(pair_item[0], pair_item[1])

    return lax.map(attend_pair, (qkv_items, bias_items))


def per_device(
    pair_map, conv_in, embed_weight, qkv_weight, key_bias, out_weight, unpatch, conv_out
):
    col_cells = pair_map.shape[1]
    row_cells = pair_map.shape[2]
    patch_cols = col_cells // PATCH
    patch_rows = row_cells // PATCH
    first_conv = convolve(pair_map, conv_in, fetch_input)
    mixed_map = (pair_map.astype(jnp.float32) + jax.nn.silu(first_conv)).astype(jnp.bfloat16)
    patches = (
        mixed_map.reshape(C, patch_cols, PATCH, patch_rows, PATCH)
        .transpose(3, 1, 0, 2, 4)
        .reshape(patch_rows * patch_cols, C * PATCH * PATCH)
    )
    tokens = jnp.dot(patches, embed_weight, preferred_element_type=jnp.float32).astype(jnp.bfloat16)
    normed = layer_norm(tokens)
    projected = jnp.dot(normed, qkv_weight, preferred_element_type=jnp.float32).astype(jnp.bfloat16)
    split_qkv = projected.reshape(patch_rows, patch_cols, 3, HEADS, HEAD_DIM)
    row_groups = lax.axis_size("rows")
    pair_share = patch_cols * HEADS // row_groups
    packed = split_qkv.transpose(1, 3, 0, 2, 4).reshape(
        row_groups, pair_share, patch_rows, 3 * HEAD_DIM
    )
    biases = key_bias.transpose(1, 2, 0).reshape(row_groups, pair_share, patch_rows)
    qkv_in = lax.all_to_all(packed, "rows", split_axis=0, concat_axis=2, tiled=True)
    bias_in = lax.all_to_all(biases, "rows", split_axis=0, concat_axis=2, tiled=True)
    outputs = attend_many(qkv_in[0], bias_in[0])
    returned = lax.all_to_all(outputs[None], "rows", split_axis=2, concat_axis=0, tiled=True)
    attended = (
        returned.reshape(patch_cols, HEADS, patch_rows, HEAD_DIM)
        .transpose(2, 0, 1, 3)
        .reshape(patch_rows * patch_cols, D)
    )
    updated = (
        tokens.astype(jnp.float32)
        + jnp.dot(attended, out_weight, preferred_element_type=jnp.float32)
    ).astype(jnp.bfloat16)
    expanded = jnp.dot(updated, unpatch, preferred_element_type=jnp.float32)
    expanded = (
        expanded.reshape(patch_rows, patch_cols, C, PATCH, PATCH)
        .transpose(2, 1, 3, 0, 4)
        .reshape(C, col_cells, row_cells)
    )
    merged = (mixed_map.astype(jnp.float32) + expanded).astype(jnp.bfloat16)
    second_conv = convolve(merged, conv_out, fetch_output)
    return (merged.astype(jnp.float32) + second_conv).astype(jnp.bfloat16)


def solution(mesh):
    placed = (P(None, "cols", "rows"), P(), P(), P(), P("rows", "cols", None), P(), P(), P())
    return jax.shard_map(
        per_device, mesh=mesh, in_specs=placed, out_specs=P(None, "cols", "rows"), check_vma=False
    )
```

profile of v0, /device:TPU:0, one launch (start us, length us, event | category | flops | bytes accessed | tf_op | source)
XLA Modules:
  0.0 172.3 jit_solution(11149883813830544106)
XLA Ops:
  0.0 1.5 fusion.36
  1.5 4.9 %collective-permute-start = (bf16[32,64,1]{2,1,0:T(8,128)(2,1)S(1)}, bf16[32,64,1]{2,1,0:T(8,128)(2,1)S(1)}, u32[]{:S(2)}, u32[]{:S(2)}) collective-permute-start(bf16[32,64,1]{2,1,0:T(8,128)(2,1)S(1)} %get-tuple-element.66), channel_id=1, source_target_pairs={{0,2},{2,4},{4,6},{6,8},{8,10},{10,12},{12,14},{14,16},{16,18},{18... | collective-permute-start | bytes 12296 | tf_op jit(solution)/shard_map/ppermute | solution.py:21
  6.5 1.4 collective-permute-start.1
  7.9 20.9 %collective-permute-done = bf16[32,64,1]{2,1,0:T(8,128)(2,1)S(1)} collective-permute-done((bf16[32,64,1]{2,1,0:T(8,128)(2,1)S(1)}, bf16[32,64,1]{2,1,0:T(8,128)(2,1)S(1)}, u32[]{:S(2)}, u32[]{:S(2)}) %collective-permute-start) | collective-permute-done | bytes 4128 | tf_op jit(solution)/shard_map/ppermute | solution.py:21
  28.8 1.9 %collective-permute-done.1 = bf16[32,64,1]{2,1,0:T(8,128)(2,1)S(1)} collective-permute-done((bf16[32,64,1]{2,1,0:T(8,128)(2,1)S(1)}, bf16[32,64,1]{2,1,0:T(8,128)(2,1)S(1)}, u32[]{:S(2)}, u32[]{:S(2)}) %collective-permute-start.1) | collective-permute-done | bytes 4128 | tf_op jit(solution)/shard_map/ppermute | solution.py:24
  30.8 1.1 pad_maximum_fusion.9
  31.9 1.3 collective-permute-start.3
  33.2 3.0 %collective-permute-start.2 = (bf16[32,1,130]{2,1,0:T(2,128)(2,1)S(1)}, bf16[32,1,130]{2,1,0:T(2,128)(2,1)S(1)}, u32[]{:S(2)}, u32[]{:S(2)}) collective-permute-start(bf16[32,1,130]{2,1,0:T(2,128)(2,1)S(1)} %get-tuple-element.63), channel_id=1, source_target_pairs={{0,1},{2,3},{4,5},{6,7},{8,9},{10,11},{12,13},{14,15},{16,17},{18,... | collective-permute-start | bytes 24968 | tf_op jit(solution)/shard_map/ppermute | solution.py:21
  36.2 5.9 %all-to-all-start.1 = ((bf16[16,4,16]{2,1,0:T(4,128)(2,1)}), bf16[16,4,16]{2,1,0:T(4,128)(2,1)S(1)}, u32[]{:S(2)}, u32[]{:S(2)}) async-start(bf16[16,4,16]{2,1,0:T(4,128)(2,1)} %bitcast.106), calls=%async_computation.1 | async-start | bytes 32768 | tf_op jit(solution)/shard_map/all_to_all | solution.py:127
  42.1 2.6 %pad_maximum_fusion = (bf16[32,65,130]{2,1,0:T(8,128)(2,1)S(1)}, bf16[32,65,130]{2,1,0:T(8,128)(2,1)S(1)}) fusion(bf16[32,1,130]{2,1,0:T(2,128)(2,1)S(1)} %collective-permute-done.3, bf16[32,64,1]{2,1,0:T(8,128)(2,1)S(1)} %collective-permute-done.1, bf16[32,64,128]{2,1,0:T(8,128)(2,1)} %param.10, bf16[32,64,1]{2,1,0:T(8,128)(2,1)S(1)} %collective-permute-done, ...), kind=kLoop, calls=%fused_computation.22 | loop fusion | flops 4326400 | bytes 1630720 | tf_op jit(solution)/shard_map/concatenate | solution.py:25
  47.8 2.8 %fusion.13 = f32[4,8,64,128]{3,1,2,0:T(8,128)S(1)} fusion(bf16[32,288]{1,0:T(8,128)(2,1)S(1)} %copy-done.6, bf16[36,8,64,128]{3,2,1,0:T(8,128)(2,1)S(1)} %bitcast.96), kind=kOutput, calls=%fused_computation.19 | convolution fusion | flops 150994944 | bytes 5785600 | tf_op jit(solution)/shard_map/dot_general | solution.py:41
  50.9 1.1 fusion.27
  52.0 2.0 %copy.115 = bf16[32,64,128]{0,2,1:T(8,128)(2,1)S(1)} copy(bf16[32,64,128]{2,1,0:T(8,128)(2,1)} %fusion.27) | data formatting | bytes 1048576 | tf_op jit(solution)/shard_map/convert_element_type | solution.py:110
  54.0 6.8 %copy.116 = bf16[16,8,32,8,8]{4,3,2,1,0:T(8,128)(2,1)} copy(bf16[16,8,32,8,8]{2,4,0,3,1:T(8,128)(2,1)S(1)} %bitcast.95) | data formatting | bytes 1048576 | tf_op jit(solution)/shard_map/transpose | solution.py:113
  60.9 12.9 %reshape.63 = bf16[128,2048]{1,0:T(8,128)(2,1)S(1)} reshape(bf16[16,8,32,8,8]{4,3,2,1,0:T(8,128)(2,1)} %copy.116) | data formatting | bytes 1048576 | tf_op jit(solution)/shard_map/reshape | solution.py:114
  75.8 1.2 reshape.65
  77.0 6.9 %all-to-all-start = ((bf16[16,4,16,96]{3,2,1,0:T(8,128)(2,1)}), bf16[16,4,16,96]{3,2,1,0:T(8,128)(2,1)S(1)}, u32[]{:S(2)}, u32[]{:S(2)}) async-start(bf16[16,4,16,96]{3,2,1,0:T(8,128)(2,1)} %reshape.65), calls=%async_computation | async-start | bytes 524288 | tf_op jit(solution)/shard_map/all_to_all | solution.py:126
  84.0 8.7 %all-to-all-done = bf16[16,4,16,96]{3,2,1,0:T(8,128)(2,1)S(1)} async-done(((bf16[16,4,16,96]{3,2,1,0:T(8,128)(2,1)}), bf16[16,4,16,96]{3,2,1,0:T(8,128)(2,1)S(1)}, u32[]{:S(2)}, u32[]{:S(2)}) %all-to-all-start) | async-done | bytes 196640 | tf_op jit(solution)/shard_map/all_to_all | solution.py:126
  92.8 2.5 %while.10 = (s32[]{:T(128)}, bf16[4,256,32]{1,2,0:T(8,128)(2,1)S(1)}, bf16[4,256,96]{2,1,0:T(8,128)(2,1)S(1)}, bf16[4,256]{1,0:T(4,128)(2,1)S(1)}, s32[]{:T(128)}) while((s32[]{:T(128)}, bf16[4,256,32]{1,2,0:T(8,128)(2,1)S(1)}, bf16[4,256,96]{2,1,0:T(8,128)(2,1)S(1)}, bf16[4,256]{1,0:T(4,128)(2,1)S(1)}, s32[]{:T(128)}) %tuple.33), condition=%wide.region_5.6_spmd, body=%wide.region_2.5_spmd.sunk | while | flops 8920834 | bytes 1105489 | solution.py:99
  95.9 10.9 %all_to_all.45 = bf16[16,2,1024]{2,1,0:T(2,128)(2,1)S(1)} all-to-all(bf16[16,2,1024]{2,1,0:T(2,128)(2,1)S(1)} %reshape.74), channel_id=1, replica_groups=mesh['rows'=16,'cols'=2] {'rows'}, dimensions={0} | all-to-all | bytes 131072 | tf_op jit(solution)/shard_map/all_to_all | solution.py:129
  107.7 11.1 %reshape.69 = f32[16,8,32,8,8]{4,3,2,1,0:T(8,128)} reshape(f32[128,2048]{1,0:T(8,128)S(1)} %fusion.21) | data formatting | bytes 2097152 | tf_op jit(solution)/shard_map/reshape | solution.py:141
  118.9 11.5 %copy.124 = f32[32,8,8,16,8]{0,4,3,2,1:T(8,128)} copy(f32[32,8,8,16,8]{4,2,0,1,3:T(8,128)} %bitcast.93) | data formatting | bytes 2097152 | tf_op jit(solution)/shard_map/transpose | solution.py:142
  130.3 3.1 %copy.125 = f32[32,64,128]{2,1,0:T(8,128)S(1)} copy(f32[32,64,128]{0,2,1:T(8,128)} %bitcast.94) | data formatting | bytes 2097152 | tf_op jit(solution)/shard_map/reshape | solution.py:143
  133.9 2.8 %collective-permute-start.4 = (bf16[32,64,1]{2,1,0:T(8,128)(2,1)S(1)}, bf16[32,64,1]{2,1,0:T(8,128)(2,1)S(1)}, u32[]{:S(2)}, u32[]{:S(2)}) collective-permute-start(bf16[32,64,1]{2,1,0:T(8,128)(2,1)S(1)} %get-tuple-element.64), channel_id=1, source_target_pairs={{0,2},{2,4},{4,6},{6,8},{8,10},{10,12},{12,14},{14,16},{16,18},{18... | collective-permute-start | bytes 12296 | tf_op jit(solution)/shard_map/ppermute | solution.py:21
  136.6 1.3 collective-permute-start.5
  137.9 18.9 %collective-permute-done.4 = bf16[32,64,1]{2,1,0:T(8,128)(2,1)S(1)} collective-permute-done((bf16[32,64,1]{2,1,0:T(8,128)(2,1)S(1)}, bf16[32,64,1]{2,1,0:T(8,128)(2,1)S(1)}, u32[]{:S(2)}, u32[]{:S(2)}) %collective-permute-start.4) | collective-permute-done | bytes 4128 | tf_op jit(solution)/shard_map/ppermute | solution.py:21
  156.9 1.6 collective-permute-done.5
  158.7 1.3 collective-permute-start.7
  160.0 3.0 %collective-permute-start.6 = (bf16[32,1,130]{2,1,0:T(2,128)(2,1)S(1)}, bf16[32,1,130]{2,1,0:T(2,128)(2,1)S(1)}, u32[]{:S(2)}, u32[]{:S(2)}) collective-permute-start(bf16[32,1,130]{2,1,0:T(2,128)(2,1)S(1)} %get-tuple-element.59), channel_id=1, source_target_pairs={{0,1},{2,3},{4,5},{6,7},{8,9},{10,11},{12,13},{14,15},{16,17},{18,... | collective-permute-start | bytes 24968 | tf_op jit(solution)/shard_map/ppermute | solution.py:21
  163.9 1.3 pad_maximum_fusion.1
  168.3 2.8 %fusion.16 = f32[4,8,64,128]{3,1,2,0:T(8,128)S(1)} fusion(bf16[32,288]{1,0:T(8,128)(2,1)S(1)} %copy-done.7, bf16[36,8,64,128]{3,2,1,0:T(8,128)(2,1)S(1)} %bitcast.97), kind=kOutput, calls=%fused_computation.20 | convolution fusion | flops 150994944 | bytes 5785600 | tf_op jit(solution)/shard_map/dot_general | solution.py:41
  171.3 1.0 fusion.22
  (84 shorter events, 13.8 us)
Async XLA Ops:
  0.0 107.3 %copy-start = (bf16[256,2048]{1,0:T(8,128)(2,1)S(1)}, bf16[256,2048]{1,0:T(8,128)(2,1)}, u32[]{:S(2)}) copy-start(bf16[256,2048]{1,0:T(8,128)(2,1)} %param.16) | copy-start | bytes 3145732
  1.5 27.3 %collective-permute-start = (bf16[32,64,1]{2,1,0:T(8,128)(2,1)S(1)}, bf16[32,64,1]{2,1,0:T(8,128)(2,1)S(1)}, u32[]{:S(2)}, u32[]{:S(2)}) collective-permute-start(bf16[32,64,1]{2,1,0:T(8,128)(2,1)S(1)} %get-tuple-element.66), channel_id=1, source_target_pairs={{0,2},{2,4},{4,6},{6,8},{8,10},{10,12},{12,14},{14,16},{16,18},{18... | collective-permute-start | bytes 12296 | tf_op jit(solution)/shard_map/ppermute | solution.py:21
  6.5 39.1 %copy-start.1 = (bf16[32,64,128]{2,1,0:T(8,128)(2,1)S(1)}, bf16[32,64,128]{2,1,0:T(8,128)(2,1)}, u32[]{:S(2)}) copy-start(bf16[32,64,128]{2,1,0:T(8,128)(2,1)} %param.10) | copy-start | bytes 1572868
  6.5 24.3 %collective-permute-start.1 = (bf16[32,64,1]{2,1,0:T(8,128)(2,1)S(1)}, bf16[32,64,1]{2,1,0:T(8,128)(2,1)S(1)}, u32[]{:S(2)}, u32[]{:S(2)}) collective-permute-start(bf16[32,64,1]{2,1,0:T(8,128)(2,1)S(1)} %get-tuple-element.67), channel_id=1, source_target_pairs={{2,0},{4,2},{6,4},{8,6},{10,8},{12,10},{14,12},{16,14},{18,16},{20... | collective-permute-start | bytes 12296 | tf_op jit(solution)/shard_map/ppermute | solution.py:24
  31.9 10.3 %collective-permute-start.3 = (bf16[32,1,130]{2,1,0:T(2,128)(2,1)S(1)}, bf16[32,1,130]{2,1,0:T(2,128)(2,1)S(1)}, u32[]{:S(2)}, u32[]{:S(2)}) collective-permute-start(bf16[32,1,130]{2,1,0:T(2,128)(2,1)S(1)} %get-tuple-element.62), channel_id=1, source_target_pairs={{1,0},{3,2},{5,4},{7,6},{9,8},{11,10},{13,12},{15,14},{17,16},{19,... | collective-permute-start | bytes 24968 | tf_op jit(solution)/shard_map/ppermute | solution.py:24
  33.2 9.0 %collective-permute-start.2 = (bf16[32,1,130]{2,1,0:T(2,128)(2,1)S(1)}, bf16[32,1,130]{2,1,0:T(2,128)(2,1)S(1)}, u32[]{:S(2)}, u32[]{:S(2)}) collective-permute-start(bf16[32,1,130]{2,1,0:T(2,128)(2,1)S(1)} %get-tuple-element.63), channel_id=1, source_target_pairs={{0,1},{2,3},{4,5},{6,7},{8,9},{10,11},{12,13},{14,15},{16,17},{18,... | collective-permute-start | bytes 24968 | tf_op jit(solution)/shard_map/ppermute | solution.py:21
  36.2 40.8 %all-to-all-start.1 = ((bf16[16,4,16]{2,1,0:T(4,128)(2,1)}), bf16[16,4,16]{2,1,0:T(4,128)(2,1)S(1)}, u32[]{:S(2)}, u32[]{:S(2)}) async-start(bf16[16,4,16]{2,1,0:T(4,128)(2,1)} %bitcast.106), calls=%async_computation.1 | async-start | bytes 32768 | tf_op jit(solution)/shard_map/all_to_all | solution.py:127
  45.2 2.6 %copy-start.6 = (bf16[32,288]{1,0:T(8,128)(2,1)S(1)}, bf16[32,288]{1,0:T(8,128)(2,1)}, u32[]{:S(2)}) copy-start(bf16[32,288]{1,0:T(8,128)(2,1)} %param.11) | copy-start | bytes 55300
  60.8 13.0 %copy-start.3 = (bf16[2048,256]{1,0:T(8,128)(2,1)S(1)}, bf16[2048,256]{1,0:T(8,128)(2,1)}, u32[]{:S(2)}) copy-start(bf16[2048,256]{1,0:T(8,128)(2,1)} %param.12) | copy-start | bytes 3145732
  60.8 13.6 %copy-start.4 = (bf16[256,768]{1,0:T(8,128)(2,1)S(1)}, bf16[256,768]{1,0:T(8,128)(2,1)}, u32[]{:S(2)}) copy-start(bf16[256,768]{1,0:T(8,128)(2,1)} %param.13) | copy-start | bytes 1179652
  77.0 15.8 %all-to-all-start = ((bf16[16,4,16,96]{3,2,1,0:T(8,128)(2,1)}), bf16[16,4,16,96]{3,2,1,0:T(8,128)(2,1)S(1)}, u32[]{:S(2)}, u32[]{:S(2)}) async-start(bf16[16,4,16,96]{3,2,1,0:T(8,128)(2,1)} %reshape.65), calls=%async_computation | async-start | bytes 524288 | tf_op jit(solution)/shard_map/all_to_all | solution.py:126
  92.7 14.5 %copy-start.5 = (bf16[256,256]{1,0:T(8,128)(2,1)S(1)}, bf16[256,256]{1,0:T(8,128)(2,1)}, u32[]{:S(2)}) copy-start(bf16[256,256]{1,0:T(8,128)(2,1)} %param.15) | copy-start | bytes 393220
  130.3 3.1 %copy-start.2 = (bf16[32,64,128]{2,1,0:T(8,128)(2,1)S(1)}, bf16[32,64,128]{2,1,0:T(8,128)(2,1)}, u32[]{:S(2)}) copy-start(bf16[32,64,128]{2,1,0:T(8,128)(2,1)} %fusion.27) | copy-start | bytes 1572868
  133.9 23.0 %collective-permute-start.4 = (bf16[32,64,1]{2,1,0:T(8,128)(2,1)S(1)}, bf16[32,64,1]{2,1,0:T(8,128)(2,1)S(1)}, u32[]{:S(2)}, u32[]{:S(2)}) collective-permute-start(bf16[32,64,1]{2,1,0:T(8,128)(2,1)S(1)} %get-tuple-element.64), channel_id=1, source_target_pairs={{0,2},{2,4},{4,6},{6,8},{8,10},{10,12},{12,14},{14,16},{16,18},{18... | collective-permute-start | bytes 12296 | tf_op jit(solution)/shard_map/ppermute | solution.py:21
  136.6 21.9 %collective-permute-start.5 = (bf16[32,64,1]{2,1,0:T(8,128)(2,1)S(1)}, bf16[32,64,1]{2,1,0:T(8,128)(2,1)S(1)}, u32[]{:S(2)}, u32[]{:S(2)}) collective-permute-start(bf16[32,64,1]{2,1,0:T(8,128)(2,1)S(1)} %get-tuple-element.65), channel_id=1, source_target_pairs={{2,0},{4,2},{6,4},{8,6},{10,8},{12,10},{14,12},{16,14},{18,16},{20... | collective-permute-start | bytes 12296 | tf_op jit(solution)/shard_map/ppermute | solution.py:24
  158.7 4.3 %collective-permute-start.7 = (bf16[32,1,130]{2,1,0:T(2,128)(2,1)S(1)}, bf16[32,1,130]{2,1,0:T(2,128)(2,1)S(1)}, u32[]{:S(2)}, u32[]{:S(2)}) collective-permute-start(bf16[32,1,130]{2,1,0:T(2,128)(2,1)S(1)} %get-tuple-element.58), channel_id=1, source_target_pairs={{1,0},{3,2},{5,4},{7,6},{9,8},{11,10},{13,12},{15,14},{17,16},{19,... | collective-permute-start | bytes 24968 | tf_op jit(solution)/shard_map/ppermute | solution.py:24
  160.0 3.9 %collective-permute-start.6 = (bf16[32,1,130]{2,1,0:T(2,128)(2,1)S(1)}, bf16[32,1,130]{2,1,0:T(2,128)(2,1)S(1)}, u32[]{:S(2)}, u32[]{:S(2)}) collective-permute-start(bf16[32,1,130]{2,1,0:T(2,128)(2,1)S(1)} %get-tuple-element.59), channel_id=1, source_target_pairs={{0,1},{2,3},{4,5},{6,7},{8,9},{10,11},{12,13},{14,15},{16,17},{18,... | collective-permute-start | bytes 24968 | tf_op jit(solution)/shard_map/ppermute | solution.py:21
  165.7 2.6 %copy-start.7 = (bf16[32,288]{1,0:T(8,128)(2,1)S(1)}, bf16[32,288]{1,0:T(8,128)(2,1)}, u32[]{:S(2)}) copy-start(bf16[32,288]{1,0:T(8,128)(2,1)} %param.17) | copy-start | bytes 55300
where the time goes:
time: 173 us; the launch traced here: 172 us
  local copies, waits for them, and re-layouts  57.5 us (33%)
  waiting for transfers between devices  53 us (31%)
  starting transfers between devices  31.9 us (18%)
  blocking collectives  10.9 us (6%)
  other arithmetic  9.72 us (6%)
  matrix products  8.77 us (5%)
    ppermute x4, waiting for transfers between devices, padded_2(): lax.ppermute(lax.slice_in_dim(block, block.shape[dim] - width, None, axis...  40.7 us
    ppermute x4, starting transfers between devices, padded_2(): lax.ppermute(lax.slice_in_dim(block, block.shape[dim] - width, None, axis...  13.7 us
    reshape x1, local copies, waits for them, and re-layouts, per_device(): patches = mixed_map.reshape(C, patch_cols, PATCH, patch_rows, PATCH).tran...  12.9 us
    transpose x1, local copies, waits for them, and re-layouts, per_device(): expanded = expanded.reshape(patch_rows, patch_cols, C, PATCH, PATCH).tran...  11.5 us
    reshape x1, local copies, waits for them, and re-layouts, per_device(): expanded.reshape(patch_rows, patch_cols, C, PATCH, PATCH)  11.1 us
    all_to_all x1, blocking collectives, per_device(): lax.all_to_all(outputs[None], 'rows', split_axis=2, concat_axis=0, tiled=...  10.9 us
    all_to_all x1, waiting for transfers between devices, per_device(): lax.all_to_all(packed, 'rows', split_axis=0, concat_axis=2, tiled=True)  8.74 us
    all_to_all x1, starting transfers between devices, per_device(): lax.all_to_all(packed, 'rows', split_axis=0, concat_axis=2, tiled=True)  6.92 us
  transfers between devices with their start and end apart: 10, of which 6 were waited for; matrix products, arithmetic and copies ran while one was open for 20% of the time, Pallas kernels for 0%

commit v1 on v0

v1 whole, which is shorter than its diff:
```python
import functools

import jax
import jax.numpy as jnp
from jax import lax
from jax.experimental import pallas as pl
from jax.experimental.pallas import tpu as pltpu
from jax.sharding import PartitionSpec as P

C = 32
PATCH = 8
D = 256
HEADS = 8
HEAD_DIM = 32
LANES = 128
EPSILON = 1e-05
F32 = jnp.float32
BF16 = jnp.bfloat16
MESH = pl.DeviceIdType.MESH
NT = (((1,), (1,)), ((), ()))
TOP = 8


def dot(a, b):
    return jnp.dot(a, b, preferred_element_type=F32)


def dot_nt(a, b):
    return lax.dot_general(a, b, NT, preferred_element_type=F32)


def iota(shape, dim):
    return lax.broadcasted_iota(jnp.int32, shape, dim)


def trunk_kernel(
    R,
    NC,
    x_ref,
    kb_ref,
    cin_ref,
    cout_ref,
    embed_hbm,
    qkv_hbm,
    outw_hbm,
    unp_hbm,
    o_ref,
    tmap,
    mixed,
    edges,
    halo,
    wide,
    embed_v,
    qkv_v,
    outw_v,
    unp_v,
    embed_i,
    unp_i,
    taps,
    sendq,
    recvq,
    sendb,
    recvb,
    sendo,
    recvo,
    load_sem,
    halo_ss,
    halo_rs,
    col_ss,
    col_rs,
    q_ss,
    q_rs,
    b_ss,
    b_rs,
    o_ss,
    o_rs,
):
    row = lax.axis_index("rows")
    col = lax.axis_index("cols")
    NP = x_ref.shape[1] // PATCH
    L = x_ref.shape[2]
    PR = L // PATCH
    CJ = C * PATCH
    groups = NP * (D // LANES)
    split = R // groups
    group_heads = LANES // HEAD_DIM
    my_heads = group_heads // split
    keys = R * PR

    loads = [
        pltpu.make_async_copy(src, dst, load_sem.at[n])
        for n, (src, dst) in enumerate(
            ((embed_hbm, embed_v), (qkv_hbm, qkv_v), (outw_hbm, outw_v), (unp_hbm, unp_v))
        )
    ]
    for copy in loads:
        copy.start()

    row_ok = {-1: row > 0, 1: row < R - 1}
    col_ok = {-1: col > 0, 0: col >= 0, 1: col < NC - 1}
    barrier = pltpu.get_barrier_semaphore()

    def greet(d, carry):
        pl.semaphore_signal(
            barrier,
            inc=1,
            device_id={"rows": lax.rem(row + d, R), "cols": col},
            device_id_type=MESH,
        )
        return carry

    lax.fori_loop(1, R, greet, 0)
    expected = R - 1
    for dc in (-1, 1):
        for dr in (-1, 0, 1):
            ok = col_ok[dc] if dr == 0 else jnp.logical_and(col_ok[dc], row_ok[dr])
            expected = expected + ok.astype(jnp.int32)

            @pl.when(ok)
            def _():
                pl.semaphore_signal(
                    barrier,
                    inc=1,
                    device_id={"rows": row + dr, "cols": col + dc},
                    device_id_type=MESH,
                )

    def put_edges(phase):
        for p in range(NP):
            edges[phase, 0, p : p + 1, :] = tmap[phase, p + 1, TOP + L - 1 : TOP + L, :]
            edges[phase, 1, p : p + 1, :] = tmap[phase, p + 1, TOP : TOP + 1, :]

    for q in range(NP // 2):
        pair = x_ref[:, 2 * PATCH * q : 2 * PATCH * (q + 1), :].astype(F32)
        for s in range(2):
            block = pair[:, PATCH * s : PATCH * (s + 1), :].reshape(CJ, L)
            tmap[0, 1 + 2 * q + s, TOP : TOP + L, :] = block.T
    put_edges(0)

    bias = kb_ref[...].astype(F32)
    for p in range(NP):
        block = jnp.concatenate(
            [bias[:, p, :], jnp.zeros((PR, LANES - HEADS), F32)], axis=1
        )
        sendb[p] = block.astype(BF16)

    for phase in range(2):
        for way, dr in ((0, -1), (1, 1)):
            for slot in range(3):
                missing = jnp.logical_not(jnp.logical_and(row_ok[dr], col_ok[slot - 1]))

                @pl.when(missing)
                def _():
                    halo[phase, way, slot] = jnp.zeros((NP, CJ), F32)

        for side, dc in ((0, -1), (1, 1)):

            @pl.when(jnp.logical_not(col_ok[dc]))
            def _():
                tmap[phase, side * (NP + 1), TOP : TOP + L, :] = jnp.zeros((L, CJ), F32)

    pl.semaphore_wait(barrier, expected)

    def halo_copies(phase, act):
        for side, dc in ((0, 1), (1, -1)):
            copy = pltpu.make_async_remote_copy(
                src_ref=tmap.at[phase, NP if side == 0 else 1, pl.ds(TOP, L)],
                dst_ref=tmap.at[phase, 0 if side == 0 else NP + 1, pl.ds(TOP, L)],
                send_sem=col_ss.at[phase, side],
                recv_sem=col_rs.at[phase, side],
                device_id={"rows": row, "cols": col + (-dc if act == "recv" else dc)},
                device_id_type=MESH,
            )
            ok = col_ok[-dc] if act == "recv" else col_ok[dc]

            @pl.when(ok)
            def _():
                if act == "start":
                    copy.start()
                elif act == "send":
                    copy.wait_send()
                else:
                    copy.wait_recv()

        for way, dr in ((0, 1), (1, -1)):
            for slot in range(3):
                dc = slot - 1
                if act == "recv":
                    ok = jnp.logical_and(row_ok[-dr], col_ok[dc])
                    peer = {"rows": row - dr, "cols": col + dc}
                else:
                    ok = jnp.logical_and(row_ok[dr], col_ok[-dc])
                    peer = {"rows": row + dr, "cols": col - dc}
                copy = pltpu.make_async_remote_copy(
                    src_ref=edges.at[phase, way],
                    dst_ref=halo.at[phase, way, slot],
                    send_sem=halo_ss.at[phase, way, slot],
                    recv_sem=halo_rs.at[phase, way, slot],
                    device_id=peer,
                    device_id_type=MESH,
                )

                @pl.when(ok)
                def _():
                    if act == "start":
                        copy.start()
                    elif act == "send":
                        copy.wait_send()
                    else:
                        copy.wait_recv()

    def exchange(act, source, target, send_sem, recv_sem):
        def step(d, carry):
            peer = lax.rem(row + d, R)
            copy = pltpu.make_async_remote_copy(
                src_ref=source(peer),
                dst_ref=target.at[peer if act == "recv" else row],
                send_sem=send_sem.at[peer],
                recv_sem=recv_sem.at[peer if act == "recv" else row],
                device_id={"rows": peer, "cols": col},
                device_id_type=MESH,
            )
            if act == "start":
                copy.start()
            elif act == "send":
                copy.wait_send()
            else:
                copy.wait_recv()
            return carry

        lax.fori_loop(1, R, step, 0)

    halo_copies(0, "start")
    heads_per_col = split * (D // LANES)
    bias_source = lambda peer: sendb.at[peer // heads_per_col]
    exchange("start", bias_source, recvb, b_ss, b_rs)
    recvb[row] = sendb[row // heads_per_col]

    spread = (iota((CJ, C), 0) // PATCH == iota((CJ, C), 1)).astype(F32).astype(BF16)
    both = jnp.concatenate(
        [dot(spread, cin_ref[...]).astype(BF16), dot(spread, cout_ref[...]).astype(BF16)], axis=0
    )
    in_place = iota((CJ, 2 * CJ), 0) % PATCH
    out_place = iota((CJ, 2 * CJ), 1) % PATCH
    channel = iota((CJ, 9 * C), 0) // PATCH
    tap = iota((CJ, 9 * C), 1)
    for b in range(3):
        centre = jnp.zeros((CJ, 2 * CJ), F32)
        rim = jnp.zeros((CJ, 2 * CJ), F32)
        for a in range(3):
            pick = (tap == channel + (3 * a + b) * C).astype(F32).astype(BF16)
            full = dot_nt(pick, both)
            centre = jnp.where(in_place == out_place + (a - 1), full, centre)
            if a == 0:
                rim = jnp.where(in_place == out_place + (PATCH - 1), full, rim)
            if a == 2:
                rim = jnp.where(in_place == out_place - (PATCH - 1), full, rim)
        for n in range(2):
            taps[n, b, 0:CJ, :] = centre[:, n * CJ : (n + 1) * CJ].astype(BF16)
            taps[n, b, CJ : 2 * CJ, :] = rim[:, n * CJ : (n + 1) * CJ].astype(BF16)

    loads[0].wait()
    for half in range(2):
        wide[half] = embed_v[:, half * LANES : (half + 1) * LANES].astype(F32)
    for i in range(PATCH):
        for half in range(2):
            embed_i[i, :, half * LANES : (half + 1) * LANES] = wide[
                half, pl.ds(i, CJ, stride=PATCH), :
            ].astype(BF16)

    lane_place = iota((1, 1, CJ), 2) % PATCH

    def conv(phase):
        halo_copies(phase, "recv")
        for way, place in ((0, TOP - 1), (1, TOP + L)):
            for p in range(NP):
                tmap[phase, p + 1, place : place + 1, :] = halo[phase, way, 1, p : p + 1, :]
            tmap[phase, 0, place : place + 1, :] = halo[phase, way, 0, NP - 1 : NP, :]
            tmap[phase, NP + 1, place : place + 1, :] = halo[phase, way, 2, 0:1, :]
        total = None
        for b in range(3):
            cells = tmap[phase, :, TOP - 1 + b : TOP - 1 + b + L, :]
            centre = cells[1 : NP + 1].reshape(NP * L, CJ).astype(BF16)
            rim = jnp.where(
                lane_place == PATCH - 1,
                cells[0:NP],
                jnp.where(lane_place == 0, cells[2 : NP + 2], 0.0),
            )
            rim = rim.reshape(NP * L, CJ).astype(BF16)
            part = dot(centre, taps[phase, b, 0:CJ, :]) + dot(rim, taps[phase, b, CJ : 2 * CJ, :])
            total = part if total is None else total + part
        return total

    first = conv(0)
    base = tmap[0, 1 : NP + 1, TOP : TOP + L, :].reshape(NP * L, CJ)
    mix = (base + first / (1.0 + jnp.exp(-first))).astype(BF16).astype(F32)
    for half in range(2):
        mixed[half] = mix[:, half * LANES : (half + 1) * LANES]

    total = None
    for i in range(PATCH):
        for half in range(2):
            cells = mixed[half, pl.ds(i, NP * PR, stride=PATCH), :].astype(BF16)
            part = dot(cells, embed_i[i, half * LANES : (half + 1) * LANES, :])
            total = part if total is None else total + part
    tokens = total.astype(BF16).astype(F32)
    mean = jnp.mean(tokens, axis=1, keepdims=True)
    centred = tokens - mean
    var = jnp.mean(centred * centred, axis=1, keepdims=True)
    normed = (centred * lax.rsqrt(var + EPSILON)).astype(BF16)
    loads[1].wait()
    projected = dot(normed, qkv_v[...]).astype(BF16)
    for g in range(D // LANES):
        for kind in range(3):
            start = kind * D + g * LANES
            part = projected[:, start : start + LANES].reshape(NP, PR, LANES)
            for p in range(NP):
                sendq[p * (D // LANES) + g, :, kind * LANES : (kind + 1) * LANES] = part[p]
    q_source = lambda peer: sendq.at[peer // split]
    exchange("start", q_source, recvq, q_ss, q_rs)
    recvq[row] = sendq[row // split]

    loads[3].wait()
    for k in range(PATCH):
        block = unp_v[:, k * CJ : (k + 1) * CJ].astype(F32).T
        for half in range(2):
            wide[half, k * CJ : (k + 1) * CJ, :] = block[:, half * LANES : (half + 1) * LANES]
    for i in range(PATCH):
        for half in range(2):
            unp_i[i, :, half * LANES : (half + 1) * LANES] = wide[
                half, pl.ds(i, CJ, stride=PATCH), :
            ].astype(BF16)

    exchange("recv", bias_source, recvb, b_ss, b_rs)
    first_head = lax.rem(row, split) * my_heads
    first_global = lax.rem(row // split, D // LANES) * group_heads + first_head
    pick = (iota((16, LANES), 1) == iota((16, LANES), 0) + first_global).astype(F32).astype(BF16)
    key_shift = dot_nt(pick, recvb[...].reshape(keys, LANES))
    exchange("recv", q_source, recvq, q_ss, q_rs)
    queries = recvq[:, :, 0:LANES].reshape(keys, LANES).astype(F32)
    key_rows = recvq[:, :, LANES : 2 * LANES].reshape(keys, LANES)
    values = recvq[:, :, 2 * LANES : 3 * LANES].reshape(keys, LANES).astype(F32)
    lane_head = iota((1, LANES), 1) // HEAD_DIM
    total = None
    for k in range(my_heads):
        mine = lane_head == first_head + k
        query = jnp.where(mine, queries, 0.0).astype(BF16)
        scores = dot_nt(query, key_rows) * (HEAD_DIM**-0.5) + key_shift[k : k + 1, :]
        weights = jnp.exp(scores - jnp.max(scores, axis=1, keepdims=True))
        soft = (weights / jnp.sum(weights, axis=1, keepdims=True)).astype(BF16)
        part = dot(soft, jnp.where(mine, values, 0.0).astype(BF16))
        total = part if total is None else total + part
    sendo[...] = total.astype(BF16).reshape(R, PR, LANES)
    o_source = lambda peer: sendo.at[peer]
    exchange("start", o_source, recvo, o_ss, o_rs)
    recvo[row] = sendo[row]
    loads[2].wait()
    exchange("send", bias_source, recvb, b_ss, b_rs)
    exchange("send", q_source, recvq, q_ss, q_rs)
    halo_copies(0, "send")
    exchange("recv", o_source, recvo, o_ss, o_rs)

    back = recvo[...].reshape(NP, D // LANES, split, PR, LANES)
    sides = []
    for g in range(D // LANES):
        share = back[:, g, 0]
        for s in range(1, split):
            share = share + back[:, g, s]
        sides.append(share.reshape(NP * PR, LANES))
    attended = jnp.concatenate(sides, axis=1)
    updated = (tokens + dot(attended, outw_v[...])).astype(BF16)
    for i in range(PATCH):
        expanded = dot_nt(updated, unp_i[i])
        for half in range(2):
            wide[half, pl.ds(i, NP * PR, stride=PATCH), :] = expanded[
                :, half * LANES : (half + 1) * LANES
            ]
    merged = jnp.concatenate(
        [mixed[half] + wide[half, 0 : NP * L, :] for half in range(2)], axis=1
    )
    merged = merged.astype(BF16).astype(F32)
    tmap[1, 1 : NP + 1, TOP : TOP + L, :] = merged.reshape(NP, L, CJ)
    put_edges(1)
    halo_copies(1, "start")
    exchange("send", o_source, recvo, o_ss, o_rs)
    second = conv(1)
    result = tmap[1, 1 : NP + 1, TOP : TOP + L, :] + second.reshape(NP, L, CJ)
    for q in range(NP // 2):
        blocks = [result[2 * q + s].T.reshape(C, PATCH, L) for s in range(2)]
        o_ref[:, 2 * PATCH * q : 2 * PATCH * (q + 1), :] = jnp.concatenate(blocks, axis=1).astype(
            BF16
        )
    halo_copies(1, "send")


def per_device(
    R, NC, pair_map, conv_in, embed_weight, qkv_weight, key_bias, out_weight, unpatch, conv_out
):
    NP = pair_map.shape[1] // PATCH
    L = pair_map.shape[2]
    PR = L // PATCH
    CJ = C * PATCH
    groups = NP * (D // LANES)
    vmem = pl.BlockSpec(memory_space=pltpu.VMEM)
    hbm = pl.BlockSpec(memory_space=pl.ANY)
    dma = pltpu.SemaphoreType.DMA
    return pl.pallas_call(
        functools.partial(trunk_kernel, R, NC),
        out_shape=jax.ShapeDtypeStruct(pair_map.shape, BF16),
        in_specs=[vmem] * 4 + [hbm] * 4,
        out_specs=vmem,
        scratch_shapes=[
            pltpu.VMEM((2, NP + 2, L + 2 * TOP, CJ), F32),
            pltpu.VMEM((2, NP * L, LANES), F32),
            pltpu.VMEM((2, 2, NP, CJ), F32),
            pltpu.VMEM((2, 2, 3, NP, CJ), F32),
            pltpu.VMEM((2, CJ * PATCH, LANES), F32),
            pltpu.VMEM(embed_weight.shape, BF16),
            pltpu.VMEM(qkv_weight.shape, BF16),
            pltpu.VMEM(out_weight.shape, BF16),
            pltpu.VMEM(unpatch.shape, BF16),
            pltpu.VMEM((PATCH, CJ, D), BF16),
            pltpu.VMEM((PATCH, CJ, D), BF16),
            pltpu.VMEM((2, 3, 2 * CJ, CJ), BF16),
            pltpu.VMEM((groups, PR, 3 * LANES), BF16),
            pltpu.VMEM((R, PR, 3 * LANES), BF16),
            pltpu.VMEM((NP, PR, LANES), BF16),
            pltpu.VMEM((R, PR, LANES), BF16),
            pltpu.VMEM((R, PR, LANES), BF16),
            pltpu.VMEM((R, PR, LANES), BF16),
            dma((4,)),
            dma((2, 2, 3)),
            dma((2, 2, 3)),
            dma((2, 2)),
            dma((2, 2)),
            dma((R,)),
            dma((R,)),
            dma((R,)),
            dma((R,)),
            dma((R,)),
            dma((R,)),
        ],
        compiler_params=pltpu.CompilerParams(
            collective_id=0, has_side_effects=True, vmem_limit_bytes=56 * 1024 * 1024
        ),
    )(
        pair_map,
        key_bias,
        conv_in,
        conv_out,
        embed_weight,
        qkv_weight,
        out_weight,
        unpatch,
    )


def solution(mesh):
    placed = (P(None, "cols", "rows"), P(), P(), P(), P("rows", "cols", None), P(), P(), P())
    return jax.shard_map(
        functools.partial(per_device, mesh.shape["rows"], mesh.shape["cols"]),
        mesh=mesh,
        in_specs=placed,
        out_specs=P(None, "cols", "rows"),
        check_vma=False,
    )
```

time: 173 us -> 37.1 us (0.21)
  local copies, waits for them, and re-layouts: 57.5 us -> 3.29 us
  waiting for transfers between devices: 53 us -> 0 us
  Pallas kernels: 0 us -> 33.5 us
  starting transfers between devices: 31.9 us -> 0 us
  blocking collectives: 10.9 us -> 0 us
  other arithmetic: 9.72 us -> 0 us
  matrix products: 8.77 us -> 0 us
    ppermute x8 -> x0, waiting for transfers between devices: 44.3 us -> none  [the longest x4 40.7 us: padded_2(): lax.ppermute(lax.slice_in_dim(block, block.shape[dim] - width, None, axis...]
    pallas_call x0 -> x1, Pallas kernels: none -> 33.5 us  [per_device(): pl.pallas_call(functools.partial(trunk_kernel, R, NC), out_shape=jax.Shap...]
    reshape x7 -> x0, local copies, waits for them, and re-layouts: 29.6 us -> none  [the longest x1 12.9 us: per_device(): patches = mixed_map.reshape(C, patch_cols, PATCH, patch_rows, PATCH).tran...]
    ppermute x8 -> x0, starting transfers between devices: 19 us -> none  [the longest x4 13.7 us: padded_2(): lax.ppermute(lax.slice_in_dim(block, block.shape[dim] - width, None, axis...]
    transpose x3 -> x0, local copies, waits for them, and re-layouts: 18.4 us -> none  [the longest x1 11.5 us: per_device(): expanded = expanded.reshape(patch_rows, patch_cols, C, PATCH, PATCH).tran...]
    all_to_all x2 -> x0, starting transfers between devices: 12.8 us -> none  [the longest x1 6.92 us: per_device(): lax.all_to_all(packed, 'rows', split_axis=0, concat_axis=2, tiled=True)]
    all_to_all x1 -> x0, blocking collectives: 10.9 us -> none  [per_device(): lax.all_to_all(outputs[None], 'rows', split_axis=2, concat_axis=0, tiled=...]
    dot_general x13 -> x0, matrix products: 8.77 us -> none  [the longest x2 5.66 us: conv_valid(): jnp.dot(weight, stacked.reshape(9 * channels, extent_one * extent_two), p...]
  transfers between devices with their start and end apart: 10 -> 0, of which waited for: 6 -> 0; matrix products, arithmetic and copies ran while one was open for 20% -> 0% of each run, Pallas kernels for 0% -> 0%
where the time goes in v1:
time: 37.1 us; the launch traced here: 36.8 us
  Pallas kernels  33.5 us (90%)
  local copies, waits for them, and re-layouts  3.29 us (9%)
    pallas_call x1, Pallas kernels, per_device(): pl.pallas_call(functools.partial(trunk_kernel, R, NC), out_shape=jax.Shap...  33.5 us
    unnamed x2, local copies, waits for them, and re-layouts  3.29 us

profile of v1, /device:TPU:0, one launch (start us, length us, event | category | flops | bytes accessed | tf_op | source)
XLA Modules:
  0.0 36.8 jit_solution(14309666330549194874)
XLA Ops:
  0.0 1.4 %copy.9.kb_ref = bf16[16,8,8]{2,1,0:T(8,128)(2,1)} copy(bf16[16,8,8]{0,2,1:T(8,128)(2,1)} %param.12) | data formatting | bytes 4096 | tf_op args[4]
  1.4 33.5 %shard_map.82 = bf16[32,64,128]{2,1,0:T(8,128)(2,1)} custom-call(bf16[32,64,128]{2,1,0:T(8,128)(2,1)} %x_ref.1, bf16[16,8,8]{2,1,0:T(8,128)(2,1)} %copy.9.kb_ref, bf16[32,288]{1,0:T(8,128)(2,1)} %cin_ref.1, bf16[32,288]{1,0:T(8,128)(2,1)} %cout_ref.1, bf16[2048,256]{1,0:T(8,128)(2,1)} %embed_hbm.1, bf16[256,768]{1,0:T(8,128)(2,1)} %qkv_hbm.1, ...), custom_call_target="tpu_custom_call" | custom-call | tf_op jit(solution)/shard_map/pallas_call | solution.py:407
  35.0 1.9 %copy.11 = bf16[32,64,128]{2,1,0:T(8,128)(2,1)} copy(bf16[32,64,128]{2,1,0:T(8,128)(2,1)} %shard_map.82) | data formatting | bytes 1048576

commit v2 on v1

--- a/solution.py
+++ b/solution.py
@@ -74,6 +74,7 @@
     b_rs,
     o_ss,
     o_rs,
+    met,
 ):
     row = lax.axis_index("rows")
     col = lax.axis_index("cols")
@@ -86,6 +87,7 @@
     group_heads = LANES // HEAD_DIM
     my_heads = group_heads // split
     keys = R * PR
+    bits = R.bit_length() - 1
 
     loads = [
         pltpu.make_async_copy(src, dst, load_sem.at[n])
@@ -100,17 +102,28 @@
     col_ok = {-1: col > 0, 0: col >= 0, 1: col < NC - 1}
     barrier = pltpu.get_barrier_semaphore()
 
-    def greet(d, carry):
+    def greet(peer_row, peer_col):
         pl.semaphore_signal(
             barrier,
             inc=1,
-            device_id={"rows": lax.rem(row + d, R), "cols": col},
+            device_id={"rows": peer_row, "cols": peer_col},
             device_id_type=MESH,
         )
-        return carry
-
-    lax.fori_loop(1, R, greet, 0)
-    expected = R - 1
+
+    def partner(k):
+        low = lax.rem(row // 2**k, 2)
+        return row + (1 - 2 * low) * 2**k
+
+    for k in range(bits):
+        greet(partner(k), col)
+    expected = bits
+    for dr in (-1, 1):
+        expected = expected + row_ok[dr].astype(jnp.int32)
+
+        @pl.when(row_ok[dr])
+        def _():
+            greet(row + dr, col)
+
     for dc in (-1, 1):
         for dr in (-1, 0, 1):
             ok = col_ok[dc] if dr == 0 else jnp.logical_and(col_ok[dc], row_ok[dr])
@@ -118,12 +131,7 @@
 
             @pl.when(ok)
             def _():
-                pl.semaphore_signal(
-                    barrier,
-                    inc=1,
-                    device_id={"rows": row + dr, "cols": col + dc},
-                    device_id_type=MESH,
-                )
+                greet(row + dr, col + dc)
 
     def put_edges(phase):
         for p in range(NP):
@@ -137,12 +145,10 @@
             tmap[0, 1 + 2 * q + s, TOP : TOP + L, :] = block.T
     put_edges(0)
 
-    bias = kb_ref[...].astype(F32)
-    for p in range(NP):
-        block = jnp.concatenate(
-            [bias[:, p, :], jnp.zeros((PR, LANES - HEADS), F32)], axis=1
-        )
-        sendb[p] = block.astype(BF16)
+    same = (iota((PR, PR), 0) == iota((PR, PR), 1)).astype(F32).astype(BF16)
+    bias = dot_nt(same, kb_ref[...].astype(F32).reshape(NP * HEADS, PR).astype(BF16))
+    pad = jnp.zeros((PR, LANES - NP * HEADS), F32)
+    sendb[...] = jnp.concatenate([bias, pad], axis=1).astype(BF16)
 
     for phase in range(2):
         for way, dr in ((0, -1), (1, 1)):
@@ -231,10 +237,16 @@
         lax.fori_loop(1, R, step, 0)
 
     halo_copies(0, "start")
-    heads_per_col = split * (D // LANES)
-    bias_source = lambda peer: sendb.at[peer // heads_per_col]
-    exchange("start", bias_source, recvb, b_ss, b_rs)
-    recvb[row] = sendb[row // heads_per_col]
+
+    def tell(k):
+        pl.semaphore_signal(
+            met.at[k], inc=1, device_id={"rows": partner(k), "cols": col}, device_id_type=MESH
+        )
+
+    def hear(k):
+        pl.semaphore_wait(met.at[k], 1)
+
+    tell(0)
 
     spread = (iota((CJ, C), 0) // PATCH == iota((CJ, C), 1)).astype(F32).astype(BF16)
     both = jnp.concatenate(
@@ -258,6 +270,9 @@
         for n in range(2):
             taps[n, b, 0:CJ, :] = centre[:, n * CJ : (n + 1) * CJ].astype(BF16)
             taps[n, b, CJ : 2 * CJ, :] = rim[:, n * CJ : (n + 1) * CJ].astype(BF16)
+        if b < 2 and b + 1 < bits:
+            hear(b)
+            tell(b + 1)
 
     loads[0].wait()
     for half in range(2):
@@ -268,6 +283,9 @@
                 half, pl.ds(i, CJ, stride=PATCH), :
             ].astype(BF16)
 
+    if bits > 3:
+        hear(2)
+        tell(3)
     lane_place = iota((1, 1, CJ), 2) % PATCH
 
     def conv(phase):
@@ -296,6 +314,14 @@
     mix = (base + first / (1.0 + jnp.exp(-first))).astype(BF16).astype(F32)
     for half in range(2):
         mixed[half] = mix[:, half * LANES : (half + 1) * LANES]
+
+    for k in range(3 if bits > 3 else bits - 1, bits):
+        hear(k)
+        if k + 1 < bits:
+            tell(k + 1)
+    bias_source = lambda peer: sendb
+    exchange("start", bias_source, recvb, b_ss, b_rs)
+    recvb[row] = sendb[...]
 
     total = None
     for i in range(PATCH):
@@ -333,7 +359,7 @@
 
     exchange("recv", bias_source, recvb, b_ss, b_rs)
     first_head = lax.rem(row, split) * my_heads
-    first_global = lax.rem(row // split, D // LANES) * group_heads + first_head
+    first_global = (row // split) * group_heads + first_head
     pick = (iota((16, LANES), 1) == iota((16, LANES), 0) + first_global).astype(F32).astype(BF16)
     key_shift = dot_nt(pick, recvb[...].reshape(keys, LANES))
     exchange("recv", q_source, recvq, q_ss, q_rs)
@@ -424,7 +450,7 @@
             pltpu.VMEM((2, 3, 2 * CJ, CJ), BF16),
             pltpu.VMEM((groups, PR, 3 * LANES), BF16),
             pltpu.VMEM((R, PR, 3 * LANES), BF16),
-            pltpu.VMEM((NP, PR, LANES), BF16),
+            pltpu.VMEM((PR, LANES), BF16),
             pltpu.VMEM((R, PR, LANES), BF16),
             pltpu.VMEM((R, PR, LANES), BF16),
             pltpu.VMEM((R, PR, LANES), BF16),
@@ -439,13 +465,14 @@
             dma((R,)),
             dma((R,)),
             dma((R,)),
+            pltpu.SemaphoreType.REGULAR((R.bit_length() - 1,)),
         ],
         compiler_params=pltpu.CompilerParams(
             collective_id=0, has_side_effects=True, vmem_limit_bytes=56 * 1024 * 1024
         ),
     )(
         pair_map,
-        key_bias,
+        key_bias.transpose(1, 2, 0),
         conv_in,
         conv_out,
         embed_weight,

time: 37.1 us -> 35.2 us (0.949)
  local copies, waits for them, and re-layouts: 3.29 us -> 1.87 us
    unnamed x2 -> x1, local copies, waits for them, and re-layouts: 3.29 us -> 1.87 us
where the time goes in v2:
time: 35.2 us; the launch traced here: 35.1 us
  Pallas kernels  33.2 us (94%)
  local copies, waits for them, and re-layouts  1.87 us (5%)
    pallas_call x1, Pallas kernels, per_device(): pl.pallas_call(functools.partial(trunk_kernel, R, NC), out_shape=jax.Shap...  33.2 us
    unnamed x1, local copies, waits for them, and re-layouts  1.87 us

profile of v2, /device:TPU:0, one launch (start us, length us, event | category | flops | bytes accessed | tf_op | source)
XLA Modules:
  0.0 35.1 jit_solution(15383286069964996128)
XLA Ops:
  0.0 33.2 %shard_map.82 = bf16[32,64,128]{2,1,0:T(8,128)(2,1)} custom-call(bf16[32,64,128]{2,1,0:T(8,128)(2,1)} %x_ref.1, bf16[8,8,16]{2,1,0:T(8,128)(2,1)} %bitcast.1, bf16[32,288]{1,0:T(8,128)(2,1)} %cin_ref.1, bf16[32,288]{1,0:T(8,128)(2,1)} %cout_ref.1, bf16[2048,256]{1,0:T(8,128)(2,1)} %embed_hbm.1, bf16[256,768]{1,0:T(8,128)(2,1)} %qkv_hbm.1, ...), custom_call_target="tpu_custom_call" | custom-call | tf_op jit(solution)/shard_map/pallas_call | solution.py:433
  33.2 1.9 %copy.10 = bf16[32,64,128]{2,1,0:T(8,128)(2,1)} copy(bf16[32,64,128]{2,1,0:T(8,128)(2,1)} %shard_map.82) | data formatting | bytes 1048576

commit v3 on v2

--- a/solution.py
+++ b/solution.py
@@ -59,8 +59,6 @@
     taps,
     sendq,
     recvq,
-    sendb,
-    recvb,
     sendo,
     recvo,
     load_sem,
@@ -70,8 +68,6 @@
     col_rs,
     q_ss,
     q_rs,
-    b_ss,
-    b_rs,
     o_ss,
     o_rs,
     met,
@@ -114,6 +110,7 @@
         low = lax.rem(row // 2**k, 2)
         return row + (1 - 2 * low) * 2**k
 
+    flips = [partner(k) - row for k in range(bits)]
     for k in range(bits):
         greet(partner(k), col)
     expected = bits
@@ -148,7 +145,9 @@
     same = (iota((PR, PR), 0) == iota((PR, PR), 1)).astype(F32).astype(BF16)
     bias = dot_nt(same, kb_ref[...].astype(F32).reshape(NP * HEADS, PR).astype(BF16))
     pad = jnp.zeros((PR, LANES - NP * HEADS), F32)
-    sendb[...] = jnp.concatenate([bias, pad], axis=1).astype(BF16)
+    bias = jnp.concatenate([bias, pad], axis=1).astype(BF16)
+    for g in range(groups):
+        sendq[g, :, 3 * LANES : 4 * LANES] = bias
 
     for phase in range(2):
         for way, dr in ((0, -1), (1, 1)):
@@ -164,6 +163,27 @@
             @pl.when(jnp.logical_not(col_ok[dc]))
             def _():
                 tmap[phase, side * (NP + 1), TOP : TOP + L, :] = jnp.zeros((L, CJ), F32)
+
+    def banded(n, weight):
+        spread = (iota((CJ, C), 0) // PATCH == iota((CJ, C), 1)).astype(F32).astype(BF16)
+        wide_weight = dot(spread, weight).astype(BF16)
+        shift = iota((CJ, CJ), 0) % PATCH - iota((CJ, CJ), 1) % PATCH
+        ahead = iota((CJ, 9 * C), 1) - iota((CJ, 9 * C), 0) // PATCH
+        for b in range(3):
+            centre = jnp.zeros((CJ, CJ), F32)
+            rim = jnp.zeros((CJ, CJ), F32)
+            for a in range(3):
+                pick = (ahead == (3 * a + b) * C).astype(F32).astype(BF16)
+                full = dot_nt(pick, wide_weight)
+                centre = jnp.where(shift == a - 1, full, centre)
+                if a == 0:
+                    rim = jnp.where(shift == PATCH - 1, full, rim)
+                if a == 2:
+                    rim = jnp.where(shift == 1 - PATCH, full, rim)
+            taps[n, b, 0:CJ, :] = centre.astype(BF16)
+            taps[n, b, CJ : 2 * CJ, :] = rim.astype(BF16)
+
+    banded(0, cin_ref[...])
 
     pl.semaphore_wait(barrier, expected)
 
@@ -216,8 +236,11 @@
                         copy.wait_recv()
 
     def exchange(act, source, target, send_sem, recv_sem):
-        def step(d, carry):
-            peer = lax.rem(row + d, R)
+        for d in range(R - 1, 0, -1):
+            peer = row
+            for k in range(bits):
+                if d // 2**k % 2:
+                    peer = peer + flips[k]
             copy = pltpu.make_async_remote_copy(
                 src_ref=source(peer),
                 dst_ref=target.at[peer if act == "recv" else row],
@@ -232,9 +255,6 @@
                 copy.wait_send()
             else:
                 copy.wait_recv()
-            return carry
-
-        lax.fori_loop(1, R, step, 0)
 
     halo_copies(0, "start")
 
@@ -247,32 +267,6 @@
         pl.semaphore_wait(met.at[k], 1)
 
     tell(0)
-
-    spread = (iota((CJ, C), 0) // PATCH == iota((CJ, C), 1)).astype(F32).astype(BF16)
-    both = jnp.concatenate(
-        [dot(spread, cin_ref[...]).astype(BF16), dot(spread, cout_ref[...]).astype(BF16)], axis=0
-    )
-    in_place = iota((CJ, 2 * CJ), 0) % PATCH
-    out_place = iota((CJ, 2 * CJ), 1) % PATCH
-    channel = iota((CJ, 9 * C), 0) // PATCH
-    tap = iota((CJ, 9 * C), 1)
-    for b in range(3):
-        centre = jnp.zeros((CJ, 2 * CJ), F32)
-        rim = jnp.zeros((CJ, 2 * CJ), F32)
-        for a in range(3):
-            pick = (tap == channel + (3 * a + b) * C).astype(F32).astype(BF16)
-            full = dot_nt(pick, both)
-            centre = jnp.where(in_place == out_place + (a - 1), full, centre)
-            if a == 0:
-                rim = jnp.where(in_place == out_place + (PATCH - 1), full, rim)
-            if a == 2:
-                rim = jnp.where(in_place == out_place - (PATCH - 1), full, rim)
-        for n in range(2):
-            taps[n, b, 0:CJ, :] = centre[:, n * CJ : (n + 1) * CJ].astype(BF16)
-            taps[n, b, CJ : 2 * CJ, :] = rim[:, n * CJ : (n + 1) * CJ].astype(BF16)
-        if b < 2 and b + 1 < bits:
-            hear(b)
-            tell(b + 1)
 
     loads[0].wait()
     for half in range(2):
@@ -282,6 +276,9 @@
             embed_i[i, :, half * LANES : (half + 1) * LANES] = wide[
                 half, pl.ds(i, CJ, stride=PATCH), :
             ].astype(BF16)
+        if i in (1, 4) and i // 3 + 1 < bits:
+            hear(i // 3)
+            tell(i // 3 + 1)
 
     if bits > 3:
         hear(2)
@@ -319,9 +316,6 @@
         hear(k)
         if k + 1 < bits:
             tell(k + 1)
-    bias_source = lambda peer: sendb
-    exchange("start", bias_source, recvb, b_ss, b_rs)
-    recvb[row] = sendb[...]
 
     total = None
     for i in range(PATCH):
@@ -357,12 +351,12 @@
                 half, pl.ds(i, CJ, stride=PATCH), :
             ].astype(BF16)
 
-    exchange("recv", bias_source, recvb, b_ss, b_rs)
+    banded(1, cout_ref[...])
+    exchange("recv", q_source, recvq, q_ss, q_rs)
     first_head = lax.rem(row, split) * my_heads
     first_global = (row // split) * group_heads + first_head
     pick = (iota((16, LANES), 1) == iota((16, LANES), 0) + first_global).astype(F32).astype(BF16)
-    key_shift = dot_nt(pick, recvb[...].reshape(keys, LANES))
-    exchange("recv", q_source, recvq, q_ss, q_rs)
+    key_shift = dot_nt(pick, recvq[:, :, 3 * LANES : 4 * LANES].reshape(keys, LANES))
     queries = recvq[:, :, 0:LANES].reshape(keys, LANES).astype(F32)
     key_rows = recvq[:, :, LANES : 2 * LANES].reshape(keys, LANES)
     values = recvq[:, :, 2 * LANES : 3 * LANES].reshape(keys, LANES).astype(F32)
@@ -381,7 +375,6 @@
     exchange("start", o_source, recvo, o_ss, o_rs)
     recvo[row] = sendo[row]
     loads[2].wait()
-    exchange("send", bias_source, recvb, b_ss, b_rs)
     exchange("send", q_source, recvq, q_ss, q_rs)
     halo_copies(0, "send")
     exchange("recv", o_source, recvo, o_ss, o_rs)
@@ -448,10 +441,8 @@
             pltpu.VMEM((PATCH, CJ, D), BF16),
             pltpu.VMEM((PATCH, CJ, D), BF16),
             pltpu.VMEM((2, 3, 2 * CJ, CJ), BF16),
-            pltpu.VMEM((groups, PR, 3 * LANES), BF16),
-            pltpu.VMEM((R, PR, 3 * LANES), BF16),
-            pltpu.VMEM((PR, LANES), BF16),
-            pltpu.VMEM((R, PR, LANES), BF16),
+            pltpu.VMEM((groups, PR, 4 * LANES), BF16),
+            pltpu.VMEM((R, PR, 4 * LANES), BF16),
             pltpu.VMEM((R, PR, LANES), BF16),
             pltpu.VMEM((R, PR, LANES), BF16),
             dma((4,)),
@@ -459,8 +450,6 @@
             dma((2, 2, 3)),
             dma((2, 2)),
             dma((2, 2)),
-            dma((R,)),
-            dma((R,)),
             dma((R,)),
             dma((R,)),
             dma((R,)),

time: 35.2 us -> 34.7 us (0.986)
  Pallas kernels: 33.2 us -> 32.6 us
    pallas_call x1, Pallas kernels: 33.2 us -> 32.6 us  [per_device(): pl.pallas_call(functools.partial(trunk_kernel, R, NC), out_shape=jax.Shap...]
where the time goes in v3:
time: 34.7 us; the launch traced here: 34.5 us
  Pallas kernels  32.6 us (94%)
  local copies, waits for them, and re-layouts  1.87 us (5%)
    pallas_call x1, Pallas kernels, per_device(): pl.pallas_call(functools.partial(trunk_kernel, R, NC), out_shape=jax.Shap...  32.6 us
    unnamed x1, local copies, waits for them, and re-layouts  1.87 us

profile of v3, /device:TPU:0, one launch (start us, length us, event | category | flops | bytes accessed | tf_op | source)
XLA Modules:
  0.0 34.5 jit_solution(12759162544831551883)
XLA Ops:
  0.0 32.6 %shard_map.82 = bf16[32,64,128]{2,1,0:T(8,128)(2,1)} custom-call(bf16[32,64,128]{2,1,0:T(8,128)(2,1)} %x_ref.1, bf16[8,8,16]{2,1,0:T(8,128)(2,1)} %bitcast.1, bf16[32,288]{1,0:T(8,128)(2,1)} %cin_ref.1, bf16[32,288]{1,0:T(8,128)(2,1)} %cout_ref.1, bf16[2048,256]{1,0:T(8,128)(2,1)} %embed_hbm.1, bf16[256,768]{1,0:T(8,128)(2,1)} %qkv_hbm.1, ...), custom_call_target="tpu_custom_call" | custom-call | tf_op jit(solution)/shard_map/pallas_call | solution.py:426
  32.6 1.9 %copy.10 = bf16[32,64,128]{2,1,0:T(8,128)(2,1)} copy(bf16[32,64,128]{2,1,0:T(8,128)(2,1)} %shard_map.82) | data formatting | bytes 1048576
